TPU v7x, 512 devices: a whole 4x4x16 slice. The times are simulated.
512 devices in a mesh: leaf: 512 (over y, x, z, core).
Axes of the slice: x: 4, y: 4, z: 16, core: 2. Of those that a mesh axis runs over, the one named last changes fastest.
Arguments:
- vectors: float32 [512, 512, 128], P('leaf'), may hold values from -6 to 6
- points: float32 [512, 3, 512], P('leaf')
- leaf_basis: float32 [512, 512, 128], P('leaf'), may hold values from -0.25 to 0.25
- transfer_leaf: float32 [512, 128, 128], P('leaf'), may hold values from -0.5 to 0.5
- transfer_pair: float32 [32768, 128], P('leaf'), may hold values from -0.5 to 0.5
- transfer_quad: float32 [16384, 128], P('leaf'), may hold values from -0.5 to 0.5
- skel_leaf: float32 [512, 3, 128], P('leaf')
- skel_pair: float32 [256, 3, 128], replicated
- skel_quad: float32 [128, 3, 128], replicated
- skel_top: float32 [64, 3, 128], replicated
- near_list: int32 [512, 16], P('leaf'), may hold values from -1 to 511, as said below
- far_leaf: int32 [512, 8], P('leaf'), may hold values from -1 to 511, as said below
- far_pair: int32 [256, 8], replicated, may hold values from -1 to 255, as said below
- far_quad: int32 [128, 8], replicated, may hold values from -1 to 127, as said below
- far_top: int32 [64, 8], replicated, may hold values from -1 to 63, as said below
Outputs:
- product: float32 [512, 512, 128], P('leaf')
Inputs may be any that keep to these rules, and one draw needn't show every extreme that they name: `near_list`: entry 0 of row l is l; the other entries are distinct leaves within 8 of l, or -1 for an unused slot. `far_leaf`: distinct leaves within 8 of the row's leaf, none of them in that leaf's row of near_list, or -1 for an unused slot. `far_pair`: distinct clusters within 4 of the row's cluster and other than it, or -1 for an unused slot. `far_quad`: distinct clusters within 4 of the row's cluster and other than it, or -1 for an unused slot. `far_top`: distinct top clusters other than the row's cluster, or -1 for an unused slot.
All inputs are finite; a program needn't handle non-finite values.
Results may differ from a plain program's by a relative error of at most 0.0003.
Values sent between devices are 32-bit elements; how exact they have to be, the bound alone decides.
A program may use at most 64 MiB of HBM per device.

v0:
```python
import jax
import jax.numpy as jnp
from jax import lax
from jax.sharding import PartitionSpec as P

REACH = 8
FAR_REACH = 4
INV_FOUR_PI = 0.07957747154594767
DELTA_SQ = 0.01
HIGHEST = lax.Precision.HIGHEST


def from_partner(value, axis, bit):
    mask = 2**bit
    pairs = [(source, source ^ mask) for source in range(lax.axis_size(axis))]
    return lax.ppermute(value, axis, pairs)


def from_behind(block, axis, distance):
    devices = range(lax.axis_size(axis))
    route = [(i - distance, i) for i in devices if i - distance in devices]
    return lax.ppermute(block, axis, route)


def kernel_block(left_pts, right_pts):
    distance = jnp.zeros((left_pts.shape[1], right_pts.shape[1]), jnp.float32)
    for axis_id in range(3):
        offset_gap = left_pts[axis_id][:, None] - right_pts[axis_id][None, :]
        distance = distance + offset_gap * offset_gap
    return INV_FOUR_PI * lax.rsqrt(distance + DELTA_SQ)


def transposed_dot(matrix, values):
    return lax.dot_general(matrix, values, (((0,), (0,)), ((), ())), precision=HIGHEST)


def listed_sum(own_coords, entries, fetcher, width):

    def advance(running, partner):
        coords, values = fetcher(jnp.maximum(partner, 0))
        contrib = jnp.dot(kernel_block(own_coords, coords), values, precision=HIGHEST)
        return (running + jnp.where(partner >= 0, contrib, 0.0), None)

    start_value = jnp.zeros((own_coords.shape[1], width), jnp.float32)
    result, _ = lax.scan(advance, start_value, entries)
    return result


def pair_total(partial_value, levels):
    for bit_index in range(levels):
        partial_value = partial_value + from_partner(partial_value, "leaf", bit_index)
    return partial_value


def join_rows(block, levels, device):
    for bit_index in range(levels):
        other = from_partner(block, "leaf", bit_index)
        upper = device // 2**bit_index % 2
        block = jnp.where(
            upper == 0, jnp.concatenate([block, other], 0), jnp.concatenate([other, block], 0)
        )
    return block


def near_window(shipped):
    gathered = []
    for distance in range(-REACH, REACH + 1):
        if distance == 0:
            gathered.append(shipped)
        else:
            gathered.append(from_behind(shipped, "leaf", -distance))
    return jnp.stack(gathered)


def coef_window(shipped):
    gathered = []
    for distance in range(-REACH, REACH + 1):
        if distance == 0:
            gathered.append(shipped)
        else:
            gathered.append(from_behind(shipped, "leaf", -distance))
    return jnp.stack(gathered)


def partner_stack(coefs, stride):
    gathered = []
    for offset in list(range(-FAR_REACH, 0)) + list(range(1, FAR_REACH + 1)):
        gathered.append(from_behind(coefs, "leaf", -offset * stride))
    stacked = jnp.stack(gathered)

    def slot_of(distance):
        return distance + FAR_REACH - (distance > 0).astype(jnp.int32)

    return (stacked, slot_of)


def middle_level(coefs, skeletons, lists, transfer_rows, above, stride, device):
    width = coefs.shape[1]
    rank_rows = coefs.shape[0] // stride
    cluster = device // stride
    member = device % stride
    own_full = lax.dynamic_index_in_dim(skeletons, cluster, 0, keepdims=False)
    own_coords = lax.dynamic_slice_in_dim(own_full, member * rank_rows, rank_rows, 1)
    stacked, slot_of = partner_stack(coefs, stride)

    def fetcher(partner):
        coords = lax.dynamic_index_in_dim(skeletons, partner, 0, keepdims=False)
        position = jnp.clip(slot_of(partner - cluster), 0, stacked.shape[0] - 1)
        return (coords, lax.dynamic_index_in_dim(stacked, position, 0, keepdims=False))

    entries = lax.dynamic_index_in_dim(lists, cluster, 0, keepdims=False)
    rows_here = listed_sum(own_coords, entries, fetcher, width) + jnp.dot(
        transfer_rows, above, precision=HIGHEST
    )
    return join_rows(rows_here, stride.bit_length() - 1, device)


def per_device(
    vectors,
    points,
    leaf_basis,
    transfer_leaf,
    transfer_pair,
    transfer_quad,
    skel_leaf,
    skel_pair,
    skel_quad,
    skel_top,
    near_list,
    far_leaf,
    far_pair,
    far_quad,
    far_top,
):
    leaf_points = vectors.shape[1]
    width = vectors.shape[2]
    rank = leaf_basis.shape[2]
    device = lax.axis_index("leaf")
    own_points = points[0]
    shipped = jnp.concatenate(
        [vectors[0], own_points.reshape(3 * leaf_points // width, width)], axis=0
    )
    near_rim = near_window(shipped)

    def near_fetch(partner):
        position = jnp.clip(partner - device + REACH, 0, 2 * REACH)
        block = lax.dynamic_index_in_dim(near_rim, position, 0, keepdims=False)
        return (block[leaf_points:].reshape(3, leaf_points), block[:leaf_points])

    near_field = listed_sum(own_points, near_list[0], near_fetch, width)
    coef_leaf = transposed_dot(leaf_basis[0], vectors[0])
    coef_pair = pair_total(transposed_dot(transfer_leaf[0], coef_leaf), 1)
    pair_rows = lax.dynamic_slice_in_dim(coef_pair, device % 2 * (rank // 2), rank // 2, 0)
    coef_quad = pair_total(transposed_dot(transfer_pair, pair_rows), 2)
    quad_rows = lax.dynamic_slice_in_dim(coef_quad, device % 4 * (rank // 4), rank // 4, 0)
    coef_top = pair_total(transposed_dot(transfer_quad, quad_rows), 3)
    top_cluster = device // 8
    top_member = device % 8
    top_rows_own = lax.dynamic_slice_in_dim(coef_top, top_member * (rank // 8), rank // 8, 0)
    top_coords = lax.dynamic_index_in_dim(skel_top, top_cluster, 0, keepdims=False)
    top_entries = lax.dynamic_index_in_dim(far_top, top_cluster, 0, keepdims=False)
    all_top = lax.all_gather(top_rows_own, "leaf", axis=0, tiled=True).reshape(-1, rank, width)

    def top_fetch(partner):
        coords = lax.dynamic_index_in_dim(skel_top, partner, 0, keepdims=False)
        return (coords, lax.dynamic_index_in_dim(all_top, partner, 0, keepdims=False))

    local_top = listed_sum(top_coords, top_entries, top_fetch, width)
    local_quad = middle_level(coef_quad, skel_quad, far_quad, transfer_quad, local_top, 4, device)
    local_pair = middle_level(coef_pair, skel_pair, far_pair, transfer_pair, local_quad, 2, device)
    leaf_ship = jnp.concatenate([coef_leaf, skel_leaf[0]], axis=0)
    leaf_rim = coef_window(leaf_ship)

    def leaf_fetch(partner):
        position = jnp.clip(partner - device + REACH, 0, 2 * REACH)
        block = lax.dynamic_index_in_dim(leaf_rim, position, 0, keepdims=False)
        return (block[rank:], block[:rank])

    local_leaf = listed_sum(skel_leaf[0], far_leaf[0], leaf_fetch, width) + jnp.dot(
        transfer_leaf[0], local_pair, precision=HIGHEST
    )
    product = near_field + jnp.dot(leaf_basis[0], local_leaf, precision=HIGHEST)
    return product[None]


def solution(mesh):
    placed = (
        P("leaf", None, None),
        P("leaf", None, None),
        P("leaf", None, None),
        P("leaf", None, None),
        P("leaf", None),
        P("leaf", None),
        P("leaf", None, None),
        P(),
        P(),
        P(),
        P("leaf", None),
        P("leaf", None),
        P(),
        P(),
        P(),
    )
    return jax.shard_map(
        per_device, mesh=mesh, in_specs=placed, out_specs=P("leaf", None, None), check_vma=False
    )
```

profile of v0, /device:TPU:1, one launch (start us, length us, event | category | flops | bytes accessed | tf_op | source)
XLA Modules:
  0.0 703.7 jit_solution(9183280712991490266)
XLA Ops:
  9.1 9.6 %collective-permute-start.16 = (f32[131,128]{1,0:T(8,128)S(1)}, f32[131,128]{1,0:T(8,128)S(1)}, u32[]{:S(2)}, u32[]{:S(2)}) collective-permute-start(f32[131,128]{1,0:T(8,128)S(1)} %pad_maximum_fusion.1), channel_id=1, source_target_pairs={{0,8},{1,9},{2,10},{3,11},{4,12},{5,13},{6,14},{7,15},{8,16},{9,17... | collective-permute-start | bytes 201224 | tf_op jit(solution)/shard_map/ppermute | solution.py:22
  18.7 9.7 %collective-permute-start.17 = (f32[131,128]{1,0:T(8,128)S(1)}, f32[131,128]{1,0:T(8,128)S(1)}, u32[]{:S(2)}, u32[]{:S(2)}) collective-permute-start(f32[131,128]{1,0:T(8,128)S(1)} %pad_maximum_fusion.1), channel_id=1, source_target_pairs={{0,7},{1,8},{2,9},{3,10},{4,11},{5,12},{6,13},{7,14},{8,15},{9,16}... | collective-permute-start | bytes 201224 | tf_op jit(solution)/shard_map/ppermute | solution.py:22
  28.4 3.6 collective-permute-start.18
  31.9 2.8 collective-permute-start.19
  35.9 2.6 collective-permute-start.32
  46.0 3.1 collective-permute-start.20
  52.5 2.5 collective-permute-start.22
  71.0 10.2 %collective-permute-start = (f32[524,128]{1,0:T(8,128)S(1)}, f32[524,128]{1,0:T(8,128)S(1)}, u32[]{:S(2)}, u32[]{:S(2)}) collective-permute-start(f32[524,128]{1,0:T(8,128)S(1)} %pad_maximum_fusion), channel_id=1, source_target_pairs={{0,8},{1,9},{2,10},{3,11},{4,12},{5,13},{6,14},{7,15},{8,16},{9,17... | collective-permute-start | bytes 804872 | tf_op jit(solution)/shard_map/ppermute | solution.py:22
  81.3 8.1 %collective-permute-start.1 = (f32[524,128]{1,0:T(8,128)S(1)}, f32[524,128]{1,0:T(8,128)S(1)}, u32[]{:S(2)}, u32[]{:S(2)}) collective-permute-start(f32[524,128]{1,0:T(8,128)S(1)} %pad_maximum_fusion), channel_id=1, source_target_pairs={{0,7},{1,8},{2,9},{3,10},{4,11},{5,12},{6,13},{7,14},{8,15},{9,16}... | collective-permute-start | bytes 804872 | tf_op jit(solution)/shard_map/ppermute | solution.py:22
  89.4 5.4 collective-permute-start.2
  94.9 10.9 %collective-permute-start.33 = (f32[128,128]{1,0:T(8,128)S(1)}, f32[128,128]{1,0:T(8,128)S(1)}, u32[]{:S(2)}, u32[]{:S(2)}) collective-permute-start(f32[128,128]{1,0:T(8,128)S(1)} %add.188), channel_id=1, source_target_pairs={{0,8},{1,9},{2,10},{3,11},{4,12},{5,13},{6,14},{7,15},{8,16},{9,17... | collective-permute-start | bytes 196616 | tf_op jit(solution)/shard_map/ppermute | solution.py:22
  105.8 4.1 collective-permute-start.34
  111.0 29.7 %while.56 = (s32[]{:T(128)}, f32[128,128]{1,0:T(8,128)S(1)}, s32[8]{0:T(128)S(1)}, f32[3,128]{1,0:T(4,128)S(1)}, s32[]{:T(128)}, /*index=5*/f32[17,131,128]{2,1,...) while((s32[]{:T(128)}, f32[128,128]{1,0:T(8,128)S(1)}, ...), condition=%wide.region_3.4_spmd.clone, body=%wide.region_2.3_spmd.clone.sunk | while | flops 25378828 | bytes 206616 | solution.py:45
  140.7 14.2 %collective-permute-start.35 = (f32[128,128]{1,0:T(8,128)S(1)}, f32[128,128]{1,0:T(8,128)S(1)}, u32[]{:S(2)}, u32[]{:S(2)}) collective-permute-start(f32[128,128]{1,0:T(8,128)S(1)} %add.188), channel_id=1, source_target_pairs={{0,4},{1,5},{2,6},{3,7},{4,8},{5,9},{6,10},{7,11},{8,12},{9,13},{1... | collective-permute-start | bytes 196616 | tf_op jit(solution)/shard_map/ppermute | solution.py:22
  156.3 3.7 collective-permute-done.35
  166.3 3.1 collective-permute-done.38
  169.4 2.9 collective-permute-start.41
  174.6 6.8 collective-permute-start.42
  181.4 2.6 collective-permute-done.40
  184.0 23.4 %while.57 = (s32[]{:T(128)}, f32[64,128]{1,0:T(8,128)S(1)}, s32[8]{0:T(128)S(1)}, f32[3,64]{1,0:T(4,128)S(1)}, f32[256,3,128]{2,0,1:T(8,128)}, /*index=5*/s32[]{...) while((s32[]{:T(128)}, f32[64,128]{1,0:T(8,128)S(1)}, ...), condition=%wide.region_5.6_spmd.clone, body=%wide.region_4.5_spmd.clone.sunk | while | flops 12689422 | bytes 139043 | solution.py:45
  207.5 17.1 %collective-permute-start.43 = (f32[128,128]{1,0:T(8,128)S(1)}, f32[128,128]{1,0:T(8,128)S(1)}, u32[]{:S(2)}, u32[]{:S(2)}) collective-permute-start(f32[128,128]{1,0:T(8,128)S(1)} %add.194), channel_id=1, source_target_pairs={{0,16},{1,17},{2,18},{3,19},{4,20},{5,21},{6,22},{7,23},{8,24},{9,... | collective-permute-start | bytes 196616 | tf_op jit(solution)/shard_map/ppermute | solution.py:22
  224.6 14.2 %collective-permute-start.44 = (f32[128,128]{1,0:T(8,128)S(1)}, f32[128,128]{1,0:T(8,128)S(1)}, u32[]{:S(2)}, u32[]{:S(2)}) collective-permute-start(f32[128,128]{1,0:T(8,128)S(1)} %add.194), channel_id=1, source_target_pairs={{0,12},{1,13},{2,14},{3,15},{4,16},{5,17},{6,18},{7,19},{8,20},{9,... | collective-permute-start | bytes 196616 | tf_op jit(solution)/shard_map/ppermute | solution.py:22
  239.1 5.7 collective-permute-start.45
  246.2 5.5 collective-permute-done.45
  259.3 3.8 collective-permute-start.52
  263.2 2.4 collective-permute-done.52
  265.6 7.7 %collective-permute-start.3 = (f32[524,128]{1,0:T(8,128)S(1)}, f32[524,128]{1,0:T(8,128)S(1)}, u32[]{:S(2)}, u32[]{:S(2)}) collective-permute-start(f32[524,128]{1,0:T(8,128)S(1)} %pad_maximum_fusion), channel_id=1, source_target_pairs={{0,5},{1,6},{2,7},{3,8},{4,9},{5,10},{6,11},{7,12},{8,13},{9,14},{... | collective-permute-start | bytes 804872 | tf_op jit(solution)/shard_map/ppermute | solution.py:22
  273.4 5.1 collective-permute-start.53
  282.1 14.0 %collective-permute-done.49 = f32[128,128]{1,0:T(8,128)S(1)} collective-permute-done((f32[128,128]{1,0:T(8,128)S(1)}, f32[128,128]{1,0:T(8,128)S(1)}, u32[]{:S(2)}, u32[]{:S(2)}) %collective-permute-start.49) | collective-permute-done | bytes 65568 | tf_op jit(solution)/shard_map/ppermute | solution.py:22
  297.4 18.9 %collective-permute-done.50 = f32[128,128]{1,0:T(8,128)S(1)} collective-permute-done((f32[128,128]{1,0:T(8,128)S(1)}, f32[128,128]{1,0:T(8,128)S(1)}, u32[]{:S(2)}, u32[]{:S(2)}) %collective-permute-start.50) | collective-permute-done | bytes 65568 | tf_op jit(solution)/shard_map/ppermute | solution.py:22
  316.2 6.7 collective-permute-start.4
  322.9 23.4 %while.58 = (s32[]{:T(128)}, f32[32,128]{1,0:T(8,128)S(1)}, s32[8]{0:T(128)S(1)}, f32[3,32]{1,0:T(4,128)S(1)}, f32[128,3,128]{2,0,1:T(8,128)}, /*index=5*/s32[]{...) while((s32[]{:T(128)}, f32[32,128]{1,0:T(8,128)S(1)}, ...), condition=%wide.region_7.8_spmd.clone, body=%wide.region_6.7_spmd.clone.sunk | while | flops 6344718 | bytes 105507 | solution.py:45
  346.3 7.0 collective-permute-start.5
  354.0 7.0 collective-permute-start.6
  364.4 2.4 collective-permute-start.8
  380.6 14.4 %collective-permute-done.10 = f32[524,128]{1,0:T(8,128)S(1)} collective-permute-done((f32[524,128]{1,0:T(8,128)S(1)}, f32[524,128]{1,0:T(8,128)S(1)}, u32[]{:S(2)}, u32[]{:S(2)}) %collective-permute-start.10) | collective-permute-done | bytes 268320 | tf_op jit(solution)/shard_map/ppermute | solution.py:22
  397.0 4.4 collective-permute-done.11
  402.1 22.4 %collective-permute-done.12 = f32[524,128]{1,0:T(8,128)S(1)} collective-permute-done((f32[524,128]{1,0:T(8,128)S(1)}, f32[524,128]{1,0:T(8,128)S(1)}, u32[]{:S(2)}, u32[]{:S(2)}) %collective-permute-start.12) | collective-permute-done | bytes 268320 | tf_op jit(solution)/shard_map/ppermute | solution.py:22
  425.3 9.3 %collective-permute-done.13 = f32[524,128]{1,0:T(8,128)S(1)} collective-permute-done((f32[524,128]{1,0:T(8,128)S(1)}, f32[524,128]{1,0:T(8,128)S(1)}, u32[]{:S(2)}, u32[]{:S(2)}) %collective-permute-start.13) | collective-permute-done | bytes 268320 | tf_op jit(solution)/shard_map/ppermute | solution.py:22
  435.3 137.0 %all-gather.2.cloned.1.call-done = f32[8192,128]{1,0:T(8,128)} async-done(((f32[16,128]{1,0:T(8,128)}), f32[8192,128]{1,0:T(8,128)}) %all-gather.2.cloned.1.call-update) | async-done | bytes 4194320 | tf_op jit(solution)/shard_map/all_gather | solution.py:162
  572.3 30.4 %while.59 = (s32[]{:T(128)}, f32[128,128]{1,0:T(8,128)S(1)}, s32[8]{0:T(128)S(1)}, f32[3,128]{1,0:T(4,128)S(1)}, f32[64,3,128]{2,0,1:T(8,128)}, /*index=5*/f32[6...) while((s32[]{:T(128)}, f32[128,128]{1,0:T(8,128)S(1)}, ...), condition=%wide.region_9.10_spmd.clone, body=%wide.region_8.9_spmd.clone.sunk | while | flops 25378824 | bytes 207036 | solution.py:45
  606.0 3.0 collective-permute-start.55
  610.9 3.3 collective-permute-start.56
  614.2 81.0 %while.55 = (s32[]{:T(128)}, f32[512,128]{1,0:T(8,128)S(1)}, s32[16]{0:T(128)S(1)}, f32[3,512]{1,0:T(4,128)S(1)}, s32[]{:T(128)}, /*index=5*/f32[17,524,128]{2,1...) while((s32[]{:T(128)}, f32[512,128]{1,0:T(8,128)S(1)}, ...), condition=%wide.region_1.2_spmd.clone, body=%wide.region_0.1_spmd.clone.sunk | while | flops 405471232 | bytes 824088 | solution.py:45
  616.9 2.4 fusion.187
  647.3 2.4 fusion.187
  657.4 2.4 fusion.187
  682.8 2.4 fusion.187
  (371 shorter events, 199.3 us)
Async XLA Ops:
  6.5 565.8 %all-gather.2.cloned.1.call-start = ((), (), s32[]{:S(2)}) async-start(), calls=%async_computation | async-start | bytes 4202496 | tf_op jit(solution)/shard_map/all_gather | solution.py:162
  9.1 41.2 %collective-permute-start.16 = (f32[131,128]{1,0:T(8,128)S(1)}, f32[131,128]{1,0:T(8,128)S(1)}, u32[]{:S(2)}, u32[]{:S(2)}) collective-permute-start(f32[131,128]{1,0:T(8,128)S(1)} %pad_maximum_fusion.1), channel_id=1, source_target_pairs={{0,8},{1,9},{2,10},{3,11},{4,12},{5,13},{6,14},{7,15},{8,16},{9,17... | collective-permute-start | bytes 201224 | tf_op jit(solution)/shard_map/ppermute | solution.py:22
  18.7 33.8 %collective-permute-start.17 = (f32[131,128]{1,0:T(8,128)S(1)}, f32[131,128]{1,0:T(8,128)S(1)}, u32[]{:S(2)}, u32[]{:S(2)}) collective-permute-start(f32[131,128]{1,0:T(8,128)S(1)} %pad_maximum_fusion.1), channel_id=1, source_target_pairs={{0,7},{1,8},{2,9},{3,10},{4,11},{5,12},{6,13},{7,14},{8,15},{9,16}... | collective-permute-start | bytes 201224 | tf_op jit(solution)/shard_map/ppermute | solution.py:22
  28.4 26.6 %collective-permute-start.18 = (f32[131,128]{1,0:T(8,128)S(1)}, f32[131,128]{1,0:T(8,128)S(1)}, u32[]{:S(2)}, u32[]{:S(2)}) collective-permute-start(f32[131,128]{1,0:T(8,128)S(1)} %pad_maximum_fusion.1), channel_id=1, source_target_pairs={{0,6},{1,7},{2,8},{3,9},{4,10},{5,11},{6,12},{7,13},{8,14},{9,15},... | collective-permute-start | bytes 201224 | tf_op jit(solution)/shard_map/ppermute | solution.py:22
  31.9 25.3 %collective-permute-start.19 = (f32[131,128]{1,0:T(8,128)S(1)}, f32[131,128]{1,0:T(8,128)S(1)}, u32[]{:S(2)}, u32[]{:S(2)}) collective-permute-start(f32[131,128]{1,0:T(8,128)S(1)} %pad_maximum_fusion.1), channel_id=1, source_target_pairs={{0,5},{1,6},{2,7},{3,8},{4,9},{5,10},{6,11},{7,12},{8,13},{9,14},{... | collective-permute-start | bytes 201224 | tf_op jit(solution)/shard_map/ppermute | solution.py:22
  35.9 10.1 %collective-permute-start.32 = (f32[128,128]{1,0:T(8,128)S(1)}, f32[128,128]{1,0:T(8,128)S(1)}, u32[]{:S(2)}, u32[]{:S(2)}) collective-permute-start(f32[128,128]{1,0:T(8,128)S(1)} %convolution_bitcast_fusion.4), channel_id=1, source_target_pairs={{0,1},{1,0},{2,3},{3,2},{4,5},{5,4},{6,7},{7,6},{8,9},{9,8},{10,11... | collective-permute-start | bytes 196616 | tf_op jit(solution)/shard_map/ppermute | solution.py:16
  46.0 13.3 %collective-permute-start.20 = (f32[131,128]{1,0:T(8,128)S(1)}, f32[131,128]{1,0:T(8,128)S(1)}, u32[]{:S(2)}, u32[]{:S(2)}) collective-permute-start(f32[131,128]{1,0:T(8,128)S(1)} %pad_maximum_fusion.1), channel_id=1, source_target_pairs={{0,4},{1,5},{2,6},{3,7},{4,8},{5,9},{6,10},{7,11},{8,12},{9,13},{1... | collective-permute-start | bytes 201224 | tf_op jit(solution)/shard_map/ppermute | solution.py:22
  50.2 10.5 %collective-permute-start.21 = (f32[131,128]{1,0:T(8,128)S(1)}, f32[131,128]{1,0:T(8,128)S(1)}, u32[]{:S(2)}, u32[]{:S(2)}) collective-permute-start(f32[131,128]{1,0:T(8,128)S(1)} %pad_maximum_fusion.1), channel_id=1, source_target_pairs={{0,3},{1,4},{2,5},{3,6},{4,7},{5,8},{6,9},{7,10},{8,11},{9,12},{10... | collective-permute-start | bytes 201224 | tf_op jit(solution)/shard_map/ppermute | solution.py:22
  52.5 9.5 %collective-permute-start.22 = (f32[131,128]{1,0:T(8,128)S(1)}, f32[131,128]{1,0:T(8,128)S(1)}, u32[]{:S(2)}, u32[]{:S(2)}) collective-permute-start(f32[131,128]{1,0:T(8,128)S(1)} %pad_maximum_fusion.1), channel_id=1, source_target_pairs={{0,2},{1,3},{2,4},{3,5},{4,6},{5,7},{6,8},{7,9},{8,10},{9,11},{10,... | collective-permute-start | bytes 201224 | tf_op jit(solution)/shard_map/ppermute | solution.py:22
  55.0 8.4 %collective-permute-start.23 = (f32[131,128]{1,0:T(8,128)S(1)}, f32[131,128]{1,0:T(8,128)S(1)}, u32[]{:S(2)}, u32[]{:S(2)}) collective-permute-start(f32[131,128]{1,0:T(8,128)S(1)} %pad_maximum_fusion.1), channel_id=1, source_target_pairs={{0,1},{1,2},{2,3},{3,4},{4,5},{5,6},{6,7},{7,8},{8,9},{9,10},{10,1... | collective-permute-start | bytes 201224 | tf_op jit(solution)/shard_map/ppermute | solution.py:22
  60.7 7.7 %collective-permute-start.26 = (f32[131,128]{1,0:T(8,128)S(1)}, f32[131,128]{1,0:T(8,128)S(1)}, u32[]{:S(2)}, u32[]{:S(2)}) collective-permute-start(f32[131,128]{1,0:T(8,128)S(1)} %pad_maximum_fusion.1), channel_id=1, source_target_pairs={{3,0},{4,1},{5,2},{6,3},{7,4},{8,5},{9,6},{10,7},{11,8},{12,9},{13... | collective-permute-start | bytes 201224 | tf_op jit(solution)/shard_map/ppermute | solution.py:22
  62.0 9.0 %collective-permute-start.27 = (f32[131,128]{1,0:T(8,128)S(1)}, f32[131,128]{1,0:T(8,128)S(1)}, u32[]{:S(2)}, u32[]{:S(2)}) collective-permute-start(f32[131,128]{1,0:T(8,128)S(1)} %pad_maximum_fusion.1), channel_id=1, source_target_pairs={{4,0},{5,1},{6,2},{7,3},{8,4},{9,5},{10,6},{11,7},{12,8},{13,9},{1... | collective-permute-start | bytes 201224 | tf_op jit(solution)/shard_map/ppermute | solution.py:22
  63.3 17.9 %collective-permute-start.28 = (f32[131,128]{1,0:T(8,128)S(1)}, f32[131,128]{1,0:T(8,128)S(1)}, u32[]{:S(2)}, u32[]{:S(2)}) collective-permute-start(f32[131,128]{1,0:T(8,128)S(1)} %pad_maximum_fusion.1), channel_id=1, source_target_pairs={{5,0},{6,1},{7,2},{8,3},{9,4},{10,5},{11,6},{12,7},{13,8},{14,9},{... | collective-permute-start | bytes 201224 | tf_op jit(solution)/shard_map/ppermute | solution.py:22
  64.7 24.7 %collective-permute-start.29 = (f32[131,128]{1,0:T(8,128)S(1)}, f32[131,128]{1,0:T(8,128)S(1)}, u32[]{:S(2)}, u32[]{:S(2)}) collective-permute-start(f32[131,128]{1,0:T(8,128)S(1)} %pad_maximum_fusion.1), channel_id=1, source_target_pairs={{6,0},{7,1},{8,2},{9,3},{10,4},{11,5},{12,6},{13,7},{14,8},{15,9},... | collective-permute-start | bytes 201224 | tf_op jit(solution)/shard_map/ppermute | solution.py:22
  66.0 28.9 %collective-permute-start.30 = (f32[131,128]{1,0:T(8,128)S(1)}, f32[131,128]{1,0:T(8,128)S(1)}, u32[]{:S(2)}, u32[]{:S(2)}) collective-permute-start(f32[131,128]{1,0:T(8,128)S(1)} %pad_maximum_fusion.1), channel_id=1, source_target_pairs={{7,0},{8,1},{9,2},{10,3},{11,4},{12,5},{13,6},{14,7},{15,8},{16,9}... | collective-permute-start | bytes 201224 | tf_op jit(solution)/shard_map/ppermute | solution.py:22
  68.4 37.4 %collective-permute-start.31 = (f32[131,128]{1,0:T(8,128)S(1)}, f32[131,128]{1,0:T(8,128)S(1)}, u32[]{:S(2)}, u32[]{:S(2)}) collective-permute-start(f32[131,128]{1,0:T(8,128)S(1)} %pad_maximum_fusion.1), channel_id=1, source_target_pairs={{8,0},{9,1},{10,2},{11,3},{12,4},{13,5},{14,6},{15,7},{16,8},{17,9... | collective-permute-start | bytes 201224 | tf_op jit(solution)/shard_map/ppermute | solution.py:22
  71.0 275.3 %collective-permute-start = (f32[524,128]{1,0:T(8,128)S(1)}, f32[524,128]{1,0:T(8,128)S(1)}, u32[]{:S(2)}, u32[]{:S(2)}) collective-permute-start(f32[524,128]{1,0:T(8,128)S(1)} %pad_maximum_fusion), channel_id=1, source_target_pairs={{0,8},{1,9},{2,10},{3,11},{4,12},{5,13},{6,14},{7,15},{8,16},{9,17... | collective-permute-start | bytes 804872 | tf_op jit(solution)/shard_map/ppermute | solution.py:22
  81.3 272.7 %collective-permute-start.1 = (f32[524,128]{1,0:T(8,128)S(1)}, f32[524,128]{1,0:T(8,128)S(1)}, u32[]{:S(2)}, u32[]{:S(2)}) collective-permute-start(f32[524,128]{1,0:T(8,128)S(1)} %pad_maximum_fusion), channel_id=1, source_target_pairs={{0,7},{1,8},{2,9},{3,10},{4,11},{5,12},{6,13},{7,14},{8,15},{9,16}... | collective-permute-start | bytes 804872 | tf_op jit(solution)/shard_map/ppermute | solution.py:22
  89.4 272.3 %collective-permute-start.2 = (f32[524,128]{1,0:T(8,128)S(1)}, f32[524,128]{1,0:T(8,128)S(1)}, u32[]{:S(2)}, u32[]{:S(2)}) collective-permute-start(f32[524,128]{1,0:T(8,128)S(1)} %pad_maximum_fusion), channel_id=1, source_target_pairs={{0,6},{1,7},{2,8},{3,9},{4,10},{5,11},{6,12},{7,13},{8,14},{9,15},... | collective-permute-start | bytes 804872 | tf_op jit(solution)/shard_map/ppermute | solution.py:22
  94.9 45.8 %collective-permute-start.33 = (f32[128,128]{1,0:T(8,128)S(1)}, f32[128,128]{1,0:T(8,128)S(1)}, u32[]{:S(2)}, u32[]{:S(2)}) collective-permute-start(f32[128,128]{1,0:T(8,128)S(1)} %add.188), channel_id=1, source_target_pairs={{0,8},{1,9},{2,10},{3,11},{4,12},{5,13},{6,14},{7,15},{8,16},{9,17... | collective-permute-start | bytes 196616 | tf_op jit(solution)/shard_map/ppermute | solution.py:22
  105.8 49.2 %collective-permute-start.34 = (f32[128,128]{1,0:T(8,128)S(1)}, f32[128,128]{1,0:T(8,128)S(1)}, u32[]{:S(2)}, u32[]{:S(2)}) collective-permute-start(f32[128,128]{1,0:T(8,128)S(1)} %add.188), channel_id=1, source_target_pairs={{0,6},{1,7},{2,8},{3,9},{4,10},{5,11},{6,12},{7,13},{8,14},{9,15},... | collective-permute-start | bytes 196616 | tf_op jit(solution)/shard_map/ppermute | solution.py:22
  140.7 19.3 %collective-permute-start.35 = (f32[128,128]{1,0:T(8,128)S(1)}, f32[128,128]{1,0:T(8,128)S(1)}, u32[]{:S(2)}, u32[]{:S(2)}) collective-permute-start(f32[128,128]{1,0:T(8,128)S(1)} %add.188), channel_id=1, source_target_pairs={{0,4},{1,5},{2,6},{3,7},{4,8},{5,9},{6,10},{7,11},{8,12},{9,13},{1... | collective-permute-start | bytes 196616 | tf_op jit(solution)/shard_map/ppermute | solution.py:22
  155.0 7.8 %collective-permute-start.36 = (f32[128,128]{1,0:T(8,128)S(1)}, f32[128,128]{1,0:T(8,128)S(1)}, u32[]{:S(2)}, u32[]{:S(2)}) collective-permute-start(f32[128,128]{1,0:T(8,128)S(1)} %add.188), channel_id=1, source_target_pairs={{0,2},{1,3},{2,4},{3,5},{4,6},{5,7},{6,8},{7,9},{8,10},{9,11},{10,... | collective-permute-start | bytes 196616 | tf_op jit(solution)/shard_map/ppermute | solution.py:22
  165.0 9.6 %collective-permute-start.39 = (f32[128,128]{1,0:T(8,128)S(1)}, f32[128,128]{1,0:T(8,128)S(1)}, u32[]{:S(2)}, u32[]{:S(2)}) collective-permute-start(f32[128,128]{1,0:T(8,128)S(1)} %add.188), channel_id=1, source_target_pairs={{6,0},{7,1},{8,2},{9,3},{10,4},{11,5},{12,6},{13,7},{14,8},{15,9},... | collective-permute-start | bytes 196616 | tf_op jit(solution)/shard_map/ppermute | solution.py:22
  173.1 10.9 %collective-permute-start.40 = (f32[128,128]{1,0:T(8,128)S(1)}, f32[128,128]{1,0:T(8,128)S(1)}, u32[]{:S(2)}, u32[]{:S(2)}) collective-permute-start(f32[128,128]{1,0:T(8,128)S(1)} %add.188), channel_id=1, source_target_pairs={{8,0},{9,1},{10,2},{11,3},{12,4},{13,5},{14,6},{15,7},{16,8},{17,9... | collective-permute-start | bytes 196616 | tf_op jit(solution)/shard_map/ppermute | solution.py:22
  174.6 32.9 %collective-permute-start.42 = (f32[128,128]{1,0:T(8,128)S(1)}, f32[128,128]{1,0:T(8,128)S(1)}, u32[]{:S(2)}, u32[]{:S(2)}) collective-permute-start(f32[128,128]{1,0:T(8,128)S(1)} %add.193), channel_id=1, source_target_pairs={{0,2},{1,3},{2,0},{3,1},{4,6},{5,7},{6,4},{7,5},{8,10},{9,11},{10,... | collective-permute-start | bytes 196616 | tf_op jit(solution)/shard_map/ppermute | solution.py:16
  207.5 31.6 %collective-permute-start.43 = (f32[128,128]{1,0:T(8,128)S(1)}, f32[128,128]{1,0:T(8,128)S(1)}, u32[]{:S(2)}, u32[]{:S(2)}) collective-permute-start(f32[128,128]{1,0:T(8,128)S(1)} %add.194), channel_id=1, source_target_pairs={{0,16},{1,17},{2,18},{3,19},{4,20},{5,21},{6,22},{7,23},{8,24},{9,... | collective-permute-start | bytes 196616 | tf_op jit(solution)/shard_map/ppermute | solution.py:22
  224.6 20.3 %collective-permute-start.44 = (f32[128,128]{1,0:T(8,128)S(1)}, f32[128,128]{1,0:T(8,128)S(1)}, u32[]{:S(2)}, u32[]{:S(2)}) collective-permute-start(f32[128,128]{1,0:T(8,128)S(1)} %add.194), channel_id=1, source_target_pairs={{0,12},{1,13},{2,14},{3,15},{4,16},{5,17},{6,18},{7,19},{8,20},{9,... | collective-permute-start | bytes 196616 | tf_op jit(solution)/shard_map/ppermute | solution.py:22
  239.1 12.6 %collective-permute-start.45 = (f32[128,128]{1,0:T(8,128)S(1)}, f32[128,128]{1,0:T(8,128)S(1)}, u32[]{:S(2)}, u32[]{:S(2)}) collective-permute-start(f32[128,128]{1,0:T(8,128)S(1)} %add.194), channel_id=1, source_target_pairs={{0,8},{1,9},{2,10},{3,11},{4,12},{5,13},{6,14},{7,15},{8,16},{9,17... | collective-permute-start | bytes 196616 | tf_op jit(solution)/shard_map/ppermute | solution.py:22
  244.8 10.0 %collective-permute-start.46 = (f32[128,128]{1,0:T(8,128)S(1)}, f32[128,128]{1,0:T(8,128)S(1)}, u32[]{:S(2)}, u32[]{:S(2)}) collective-permute-start(f32[128,128]{1,0:T(8,128)S(1)} %add.194), channel_id=1, source_target_pairs={{0,4},{1,5},{2,6},{3,7},{4,8},{5,9},{6,10},{7,11},{8,12},{9,13},{1... | collective-permute-start | bytes 196616 | tf_op jit(solution)/shard_map/ppermute | solution.py:22
  251.7 7.6 %collective-permute-start.47 = (f32[128,128]{1,0:T(8,128)S(1)}, f32[128,128]{1,0:T(8,128)S(1)}, u32[]{:S(2)}, u32[]{:S(2)}) collective-permute-start(f32[128,128]{1,0:T(8,128)S(1)} %add.194), channel_id=1, source_target_pairs={{4,0},{5,1},{6,2},{7,3},{8,4},{9,5},{10,6},{11,7},{12,8},{13,9},{1... | collective-permute-start | bytes 196616 | tf_op jit(solution)/shard_map/ppermute | solution.py:22
  258.0 15.3 %collective-permute-start.48 = (f32[128,128]{1,0:T(8,128)S(1)}, f32[128,128]{1,0:T(8,128)S(1)}, u32[]{:S(2)}, u32[]{:S(2)}) collective-permute-start(f32[128,128]{1,0:T(8,128)S(1)} %add.194), channel_id=1, source_target_pairs={{8,0},{9,1},{10,2},{11,3},{12,4},{13,5},{14,6},{15,7},{16,8},{17,9... | collective-permute-start | bytes 196616 | tf_op jit(solution)/shard_map/ppermute | solution.py:22
  265.6 98.8 %collective-permute-start.3 = (f32[524,128]{1,0:T(8,128)S(1)}, f32[524,128]{1,0:T(8,128)S(1)}, u32[]{:S(2)}, u32[]{:S(2)}) collective-permute-start(f32[524,128]{1,0:T(8,128)S(1)} %pad_maximum_fusion), channel_id=1, source_target_pairs={{0,5},{1,6},{2,7},{3,8},{4,9},{5,10},{6,11},{7,12},{8,13},{9,14},{... | collective-permute-start | bytes 804872 | tf_op jit(solution)/shard_map/ppermute | solution.py:22
  280.1 15.9 %collective-permute-start.49 = (f32[128,128]{1,0:T(8,128)S(1)}, f32[128,128]{1,0:T(8,128)S(1)}, u32[]{:S(2)}, u32[]{:S(2)}) collective-permute-start(f32[128,128]{1,0:T(8,128)S(1)} %add.194), channel_id=1, source_target_pairs={{12,0},{13,1},{14,2},{15,3},{16,4},{17,5},{18,6},{19,7},{20,8},{21... | collective-permute-start | bytes 196616 | tf_op jit(solution)/shard_map/ppermute | solution.py:22
  296.1 20.2 %collective-permute-start.50 = (f32[128,128]{1,0:T(8,128)S(1)}, f32[128,128]{1,0:T(8,128)S(1)}, u32[]{:S(2)}, u32[]{:S(2)}) collective-permute-start(f32[128,128]{1,0:T(8,128)S(1)} %add.194), channel_id=1, source_target_pairs={{16,0},{17,1},{18,2},{19,3},{20,4},{21,5},{22,6},{23,7},{24,8},{25... | collective-permute-start | bytes 196616 | tf_op jit(solution)/shard_map/ppermute | solution.py:22
  316.2 51.3 %collective-permute-start.4 = (f32[524,128]{1,0:T(8,128)S(1)}, f32[524,128]{1,0:T(8,128)S(1)}, u32[]{:S(2)}, u32[]{:S(2)}) collective-permute-start(f32[524,128]{1,0:T(8,128)S(1)} %pad_maximum_fusion), channel_id=1, source_target_pairs={{0,4},{1,5},{2,6},{3,7},{4,8},{5,9},{6,10},{7,11},{8,12},{9,13},{1... | collective-permute-start | bytes 804872 | tf_op jit(solution)/shard_map/ppermute | solution.py:22
  346.3 23.2 %collective-permute-start.5 = (f32[524,128]{1,0:T(8,128)S(1)}, f32[524,128]{1,0:T(8,128)S(1)}, u32[]{:S(2)}, u32[]{:S(2)}) collective-permute-start(f32[524,128]{1,0:T(8,128)S(1)} %pad_maximum_fusion), channel_id=1, source_target_pairs={{0,3},{1,4},{2,5},{3,6},{4,7},{5,8},{6,9},{7,10},{8,11},{9,12},{10... | collective-permute-start | bytes 804872 | tf_op jit(solution)/shard_map/ppermute | solution.py:22
  354.0 17.6 %collective-permute-start.6 = (f32[524,128]{1,0:T(8,128)S(1)}, f32[524,128]{1,0:T(8,128)S(1)}, u32[]{:S(2)}, u32[]{:S(2)}) collective-permute-start(f32[524,128]{1,0:T(8,128)S(1)} %pad_maximum_fusion), channel_id=1, source_target_pairs={{0,2},{1,3},{2,4},{3,5},{4,6},{5,7},{6,8},{7,9},{8,10},{9,11},{10,... | collective-permute-start | bytes 804872 | tf_op jit(solution)/shard_map/ppermute | solution.py:22
  361.7 12.0 %collective-permute-start.7 = (f32[524,128]{1,0:T(8,128)S(1)}, f32[524,128]{1,0:T(8,128)S(1)}, u32[]{:S(2)}, u32[]{:S(2)}) collective-permute-start(f32[524,128]{1,0:T(8,128)S(1)} %pad_maximum_fusion), channel_id=1, source_target_pairs={{0,1},{1,2},{2,3},{3,4},{4,5},{5,6},{6,7},{7,8},{8,9},{9,10},{10,1... | collective-permute-start | bytes 804872 | tf_op jit(solution)/shard_map/ppermute | solution.py:22
  364.4 12.1 %collective-permute-start.8 = (f32[524,128]{1,0:T(8,128)S(1)}, f32[524,128]{1,0:T(8,128)S(1)}, u32[]{:S(2)}, u32[]{:S(2)}) collective-permute-start(f32[524,128]{1,0:T(8,128)S(1)} %pad_maximum_fusion), channel_id=1, source_target_pairs={{1,0},{2,1},{3,2},{4,3},{5,4},{6,5},{7,6},{8,7},{9,8},{10,9},{11,1... | collective-permute-start | bytes 804872 | tf_op jit(solution)/shard_map/ppermute | solution.py:22
  367.5 11.0 %collective-permute-start.9 = (f32[524,128]{1,0:T(8,128)S(1)}, f32[524,128]{1,0:T(8,128)S(1)}, u32[]{:S(2)}, u32[]{:S(2)}) collective-permute-start(f32[524,128]{1,0:T(8,128)S(1)} %pad_maximum_fusion), channel_id=1, source_target_pairs={{2,0},{3,1},{4,2},{5,3},{6,4},{7,5},{8,6},{9,7},{10,8},{11,9},{12,... | collective-permute-start | bytes 804872 | tf_op jit(solution)/shard_map/ppermute | solution.py:22
  369.5 25.5 %collective-permute-start.10 = (f32[524,128]{1,0:T(8,128)S(1)}, f32[524,128]{1,0:T(8,128)S(1)}, u32[]{:S(2)}, u32[]{:S(2)}) collective-permute-start(f32[524,128]{1,0:T(8,128)S(1)} %pad_maximum_fusion), channel_id=1, source_target_pairs={{3,0},{4,1},{5,2},{6,3},{7,4},{8,5},{9,6},{10,7},{11,8},{12,9},{13... | collective-permute-start | bytes 804872 | tf_op jit(solution)/shard_map/ppermute | solution.py:22
  371.6 29.8 %collective-permute-start.11 = (f32[524,128]{1,0:T(8,128)S(1)}, f32[524,128]{1,0:T(8,128)S(1)}, u32[]{:S(2)}, u32[]{:S(2)}) collective-permute-start(f32[524,128]{1,0:T(8,128)S(1)} %pad_maximum_fusion), channel_id=1, source_target_pairs={{4,0},{5,1},{6,2},{7,3},{8,4},{9,5},{10,6},{11,7},{12,8},{13,9},{1... | collective-permute-start | bytes 804872 | tf_op jit(solution)/shard_map/ppermute | solution.py:22
  373.7 50.8 %collective-permute-start.12 = (f32[524,128]{1,0:T(8,128)S(1)}, f32[524,128]{1,0:T(8,128)S(1)}, u32[]{:S(2)}, u32[]{:S(2)}) collective-permute-start(f32[524,128]{1,0:T(8,128)S(1)} %pad_maximum_fusion), channel_id=1, source_target_pairs={{5,0},{6,1},{7,2},{8,3},{9,4},{10,5},{11,6},{12,7},{13,8},{14,9},{... | collective-permute-start | bytes 804872 | tf_op jit(solution)/shard_map/ppermute | solution.py:22
  376.5 58.1 %collective-permute-start.13 = (f32[524,128]{1,0:T(8,128)S(1)}, f32[524,128]{1,0:T(8,128)S(1)}, u32[]{:S(2)}, u32[]{:S(2)}) collective-permute-start(f32[524,128]{1,0:T(8,128)S(1)} %pad_maximum_fusion), channel_id=1, source_target_pairs={{6,0},{7,1},{8,2},{9,3},{10,4},{11,5},{12,6},{13,7},{14,8},{15,9},... | collective-permute-start | bytes 804872 | tf_op jit(solution)/shard_map/ppermute | solution.py:22
  378.5 226.6 %collective-permute-start.14 = (f32[524,128]{1,0:T(8,128)S(1)}, f32[524,128]{1,0:T(8,128)S(1)}, u32[]{:S(2)}, u32[]{:S(2)}) collective-permute-start(f32[524,128]{1,0:T(8,128)S(1)} %pad_maximum_fusion), channel_id=1, source_target_pairs={{7,0},{8,1},{9,2},{10,3},{11,4},{12,5},{13,6},{14,7},{15,8},{16,9}... | collective-permute-start | bytes 804872 | tf_op jit(solution)/shard_map/ppermute | solution.py:22
  395.0 214.1 %collective-permute-start.15 = (f32[524,128]{1,0:T(8,128)S(1)}, f32[524,128]{1,0:T(8,128)S(1)}, u32[]{:S(2)}, u32[]{:S(2)}) collective-permute-start(f32[524,128]{1,0:T(8,128)S(1)} %pad_maximum_fusion), channel_id=1, source_target_pairs={{8,0},{9,1},{10,2},{11,3},{12,4},{13,5},{14,6},{15,7},{16,8},{17,9... | collective-permute-start | bytes 804872 | tf_op jit(solution)/shard_map/ppermute | solution.py:22
  610.9 84.5 %collective-permute-start.56 = (f32[64,128]{1,0:T(8,128)S(1)}, f32[64,128]{1,0:T(8,128)S(1)}, u32[]{:S(2)}, u32[]{:S(2)}) collective-permute-start(f32[64,128]{1,0:T(8,128)S(1)} %add.202), channel_id=1, source_target_pairs={{0,1},{1,0},{2,3},{3,2},{4,5},{5,4},{6,7},{7,6},{8,9},{9,8},{10,11... | collective-permute-start | bytes 98312 | tf_op jit(solution)/shard_map/ppermute | solution.py:16
  (18 other events, 1114.7 us)
Sparse Core Ops, SparseCore 0:
  282.2 290.0 all-gather.1
where the time goes:
time: 710 us; the launch traced here: 704 us
  waiting for transfers between devices  249 us (35%)
  starting transfers between devices  223 us (31%)
  local copies, waits for them, and re-layouts  85.7 us (12%)
  matrix products  64.8 us (9%)
  loops' own time  63 us (9%)
  between operations  14.7 us (2%)
    ppermute x48, starting transfers between devices, from_behind(): return lax.ppermute(block, axis, route)  191 us
    all_gather x1, waiting for transfers between devices, per_device(): lax.all_gather(top_rows_own, 'leaf', axis=0, tiled=True)  137 us
    ppermute x48, waiting for transfers between devices, from_behind(): return lax.ppermute(block, axis, route)  105 us
    another operation x5, loops' own time, listed_sum(): result, _ = lax.scan(advance, start_value, entries)  63 us
    dot_general x48, matrix products, advance(): jnp.dot(kernel_block(own_coords, coords), values, precision=HIGHEST)  59.8 us
    sub x80, local copies, waits for them, and re-layouts, kernel_block(): offset_gap = left_pts[axis_id][:, None] - right_pts[axis_id][None, :]  36.6 us
    ppermute x9, starting transfers between devices, from_partner(): return lax.ppermute(value, axis, pairs)  32 us
    dynamic_slice x48, local copies, waits for them, and re-layouts, listed_sum(): result, _ = lax.scan(advance, start_value, entries)  28.5 us
  transfers between devices with their start and end apart: 58, of which 23 were waited for; matrix products, arithmetic and copies ran while one was open for 21% of the time, Pallas kernels for 0%

commit v1 on v0

--- a/solution.py
+++ b/solution.py
@@ -159,7 +159,9 @@
     top_rows_own = lax.dynamic_slice_in_dim(coef_top, top_member * (rank // 8), rank // 8, 0)
     top_coords = lax.dynamic_index_in_dim(skel_top, top_cluster, 0, keepdims=False)
     top_entries = lax.dynamic_index_in_dim(far_top, top_cluster, 0, keepdims=False)
-    all_top = lax.all_gather(top_rows_own, "leaf", axis=0, tiled=True).reshape(-1, rank, width)
+    all_top = jnp.concatenate(
+        lax.all_to_all(jnp.stack([top_rows_own] * lax.axis_size("leaf")), "leaf", 0, 0), axis=0
+    ).reshape(-1, rank, width)
 
     def top_fetch(partner):
         coords = lax.dynamic_index_in_dim(skel_top, partner, 0, keepdims=False)

time: 710 us -> 848 us (1.19)
  the two profiles are of different devices: /device:TPU:1 before, /device:TPU:399 now
where the time goes in v1:
time: 848 us; the launch traced here: 842 us
  waiting for transfers between devices  353 us (42%)
  starting transfers between devices  269 us (32%)
  local copies, waits for them, and re-layouts  87.9 us (10%)
  matrix products  64.7 us (8%)
  loops' own time  62.8 us (7%)
    ppermute x48, waiting for transfers between devices, from_behind(): return lax.ppermute(block, axis, route)  292 us
    ppermute x48, starting transfers between devices, from_behind(): return lax.ppermute(block, axis, route)  196 us
    another operation x5, loops' own time, listed_sum(): result, _ = lax.scan(advance, start_value, entries)  62.8 us
    ppermute x9, waiting for transfers between devices, from_partner(): return lax.ppermute(value, axis, pairs)  61.1 us
    dot_general x48, matrix products, advance(): jnp.dot(kernel_block(own_coords, coords), values, precision=HIGHEST)  59.8 us
    ppermute x9, starting transfers between devices, from_partner(): return lax.ppermute(value, axis, pairs)  42.5 us
    sub x80, local copies, waits for them, and re-layouts, kernel_block(): offset_gap = left_pts[axis_id][:, None] - right_pts[axis_id][None, :]  36.5 us
    all_to_all x1, starting transfers between devices, per_device(): lax.all_to_all(jnp.stack([top_rows_own] * lax.axis_size('leaf')), 'leaf',...  30.6 us
  transfers between devices with their start and end apart: 58, of which 23 were waited for; matrix products, arithmetic and copies ran while one was open for 18% of the time, Pallas kernels for 0%

profile of v1, /device:TPU:399, one launch (start us, length us, event | category | flops | bytes accessed | tf_op | source)
XLA Modules:
  0.0 842.0 jit_solution(15027906183839901300)
XLA Ops:
  4.5 5.4 collective-permute-start.17
  9.9 6.3 collective-permute-start.18
  16.1 4.9 collective-permute-start.19
  47.1 3.8 collective-permute-start.25
  51.0 3.9 collective-permute-start.26
  54.9 4.3 collective-permute-start.27
  63.9 5.8 collective-permute-start.30
  69.7 6.0 collective-permute-start.31
  78.9 6.2 collective-permute-start
  87.4 29.6 %collective-permute-done.42 = f32[128,128]{1,0:T(8,128)S(1)} collective-permute-done((f32[128,128]{1,0:T(8,128)S(1)}, f32[128,128]{1,0:T(8,128)S(1)}, u32[]{:S(2)}, u32[]{:S(2)}) %collective-permute-start.42) | collective-permute-done | bytes 65568 | tf_op jit(solution)/shard_map/ppermute | solution.py:16
  124.5 4.1 collective-permute-start.52
  128.7 14.6 %collective-permute-done.52 = f32[128,128]{1,0:T(8,128)S(1)} collective-permute-done((f32[128,128]{1,0:T(8,128)S(1)}, f32[128,128]{1,0:T(8,128)S(1)}, u32[]{:S(2)}, u32[]{:S(2)}) %collective-permute-start.52) | collective-permute-done | bytes 65568 | tf_op jit(solution)/shard_map/ppermute | solution.py:16
  143.3 14.2 %collective-permute-start.3 = (f32[524,128]{1,0:T(8,128)S(1)}, f32[524,128]{1,0:T(8,128)S(1)}, u32[]{:S(2)}, u32[]{:S(2)}) collective-permute-start(f32[524,128]{1,0:T(8,128)S(1)} %pad_maximum_fusion), channel_id=1, source_target_pairs={{0,5},{1,6},{2,7},{3,8},{4,9},{5,10},{6,11},{7,12},{8,13},{9,14},{... | collective-permute-start | bytes 804872 | tf_op jit(solution)/shard_map/ppermute | solution.py:22
  157.5 3.5 collective-permute-start.53
  161.1 12.7 %collective-permute-done.53 = f32[128,128]{1,0:T(8,128)S(1)} collective-permute-done((f32[128,128]{1,0:T(8,128)S(1)}, f32[128,128]{1,0:T(8,128)S(1)}, u32[]{:S(2)}, u32[]{:S(2)}) %collective-permute-start.53) | collective-permute-done | bytes 65568 | tf_op jit(solution)/shard_map/ppermute | solution.py:16
  178.1 30.6 %all-to-all-start = ((f32[512,16,128]{2,1,0:T(8,128)}), f32[512,16,128]{2,1,0:T(8,128)}, u32[]{:S(2)}, u32[]{:S(2)}) async-start(f32[512,16,128]{2,1,0:T(8,128)} %stack.164), calls=%async_computation | async-start | bytes 8388608 | tf_op jit(solution)/shard_map/all_to_all | solution.py:163
  208.8 29.7 %while.56 = (s32[]{:T(128)}, f32[128,128]{1,0:T(8,128)S(1)}, s32[8]{0:T(128)S(1)}, f32[3,128]{1,0:T(4,128)S(1)}, s32[]{:T(128)}, /*index=5*/f32[17,131,128]{2,1,...) while((s32[]{:T(128)}, f32[128,128]{1,0:T(8,128)S(1)}, ...), condition=%wide.region_3.4_spmd.clone, body=%wide.region_2.3_spmd.clone.sunk | while | flops 25378828 | bytes 206616 | solution.py:45
  241.5 148.5 %collective-permute-done.34 = f32[128,128]{1,0:T(8,128)S(1)} collective-permute-done((f32[128,128]{1,0:T(8,128)S(1)}, f32[128,128]{1,0:T(8,128)S(1)}, u32[]{:S(2)}, u32[]{:S(2)}) %collective-permute-start.34) | collective-permute-done | bytes 65568 | tf_op jit(solution)/shard_map/ppermute | solution.py:22
  393.2 4.7 collective-permute-done.35
  399.9 4.3 collective-permute-done.36
  411.1 4.4 collective-permute-done.38
  418.0 13.7 %collective-permute-done.39 = f32[128,128]{1,0:T(8,128)S(1)} collective-permute-done((f32[128,128]{1,0:T(8,128)S(1)}, f32[128,128]{1,0:T(8,128)S(1)}, u32[]{:S(2)}, u32[]{:S(2)}) %collective-permute-start.39) | collective-permute-done | bytes 65568 | tf_op jit(solution)/shard_map/ppermute | solution.py:22
  433.7 10.0 %collective-permute-done.40 = f32[128,128]{1,0:T(8,128)S(1)} collective-permute-done((f32[128,128]{1,0:T(8,128)S(1)}, f32[128,128]{1,0:T(8,128)S(1)}, u32[]{:S(2)}, u32[]{:S(2)}) %collective-permute-start.40) | collective-permute-done | bytes 65568 | tf_op jit(solution)/shard_map/ppermute | solution.py:22
  445.6 23.5 %while.57 = (s32[]{:T(128)}, f32[64,128]{1,0:T(8,128)S(1)}, s32[8]{0:T(128)S(1)}, f32[3,64]{1,0:T(4,128)S(1)}, f32[256,3,128]{2,0,1:T(8,128)}, /*index=5*/s32[]{...) while((s32[]{:T(128)}, f32[64,128]{1,0:T(8,128)S(1)}, ...), condition=%wide.region_5.6_spmd.clone, body=%wide.region_4.5_spmd.clone.sunk | while | flops 12689422 | bytes 139043 | solution.py:45
  469.0 6.5 collective-permute-start.44
  475.5 7.1 collective-permute-done.44
  482.7 7.8 collective-permute-start.45
  490.4 4.3 collective-permute-done.45
  497.2 5.4 collective-permute-done.46
  502.6 3.8 collective-permute-start.47
  506.5 4.5 collective-permute-done.47
  511.0 4.9 collective-permute-start.48
  515.9 8.1 collective-permute-done.48
  526.0 11.8 %collective-permute-done.49 = f32[128,128]{1,0:T(8,128)S(1)} collective-permute-done((f32[128,128]{1,0:T(8,128)S(1)}, f32[128,128]{1,0:T(8,128)S(1)}, u32[]{:S(2)}, u32[]{:S(2)}) %collective-permute-start.49) | collective-permute-done | bytes 65568 | tf_op jit(solution)/shard_map/ppermute | solution.py:22
  539.7 14.8 %collective-permute-done.50 = f32[128,128]{1,0:T(8,128)S(1)} collective-permute-done((f32[128,128]{1,0:T(8,128)S(1)}, f32[128,128]{1,0:T(8,128)S(1)}, u32[]{:S(2)}, u32[]{:S(2)}) %collective-permute-start.50) | collective-permute-done | bytes 65568 | tf_op jit(solution)/shard_map/ppermute | solution.py:22
  554.5 13.4 %collective-permute-start.4 = (f32[524,128]{1,0:T(8,128)S(1)}, f32[524,128]{1,0:T(8,128)S(1)}, u32[]{:S(2)}, u32[]{:S(2)}) collective-permute-start(f32[524,128]{1,0:T(8,128)S(1)} %pad_maximum_fusion), channel_id=1, source_target_pairs={{0,4},{1,5},{2,6},{3,7},{4,8},{5,9},{6,10},{7,11},{8,12},{9,13},{1... | collective-permute-start | bytes 804872 | tf_op jit(solution)/shard_map/ppermute | solution.py:22
  568.0 23.3 %while.58 = (s32[]{:T(128)}, f32[32,128]{1,0:T(8,128)S(1)}, s32[8]{0:T(128)S(1)}, f32[3,32]{1,0:T(4,128)S(1)}, f32[128,3,128]{2,0,1:T(8,128)}, /*index=5*/s32[]{...) while((s32[]{:T(128)}, f32[32,128]{1,0:T(8,128)S(1)}, ...), condition=%wide.region_7.8_spmd.clone, body=%wide.region_6.7_spmd.clone.sunk | while | flops 6344718 | bytes 105507 | solution.py:45
  591.3 16.4 %collective-permute-start.5 = (f32[524,128]{1,0:T(8,128)S(1)}, f32[524,128]{1,0:T(8,128)S(1)}, u32[]{:S(2)}, u32[]{:S(2)}) collective-permute-start(f32[524,128]{1,0:T(8,128)S(1)} %pad_maximum_fusion), channel_id=1, source_target_pairs={{0,3},{1,4},{2,5},{3,6},{4,7},{5,8},{6,9},{7,10},{8,11},{9,12},{10... | collective-permute-start | bytes 804872 | tf_op jit(solution)/shard_map/ppermute | solution.py:22
  608.4 6.3 collective-permute-start.6
  621.4 4.5 collective-permute-start.9
  626.6 3.5 collective-permute-start.10
  642.3 5.8 collective-permute-start.15
  649.5 42.8 %collective-permute-done.12 = f32[524,128]{1,0:T(8,128)S(1)} collective-permute-done((f32[524,128]{1,0:T(8,128)S(1)}, f32[524,128]{1,0:T(8,128)S(1)}, u32[]{:S(2)}, u32[]{:S(2)}) %collective-permute-start.12) | collective-permute-done | bytes 268320 | tf_op jit(solution)/shard_map/ppermute | solution.py:22
  693.0 4.7 collective-permute-done.13
  698.5 28.6 %while.59 = (s32[]{:T(128)}, f32[128,128]{1,0:T(8,128)S(1)}, s32[8]{0:T(128)S(1)}, f32[3,128]{1,0:T(4,128)S(1)}, f32[64,3,128]{2,0,1:T(8,128)}, /*index=5*/f32[6...) while((s32[]{:T(128)}, f32[128,128]{1,0:T(8,128)S(1)}, ...), condition=%wide.region_9.10_spmd.clone, body=%wide.region_8.9_spmd.clone.sunk | while | flops 25378824 | bytes 207036 | solution.py:45
  727.3 20.4 %collective-permute-start.54 = (f32[32,128]{1,0:T(8,128)S(1)}, f32[32,128]{1,0:T(8,128)S(1)}, u32[]{:S(2)}, u32[]{:S(2)}) collective-permute-start(f32[32,128]{1,0:T(8,128)S(1)} %add.201), channel_id=1, source_target_pairs={{0,1},{1,0},{2,3},{3,2},{4,5},{5,4},{6,7},{7,6},{8,9},{9,8},{10,11... | collective-permute-start | bytes 49160 | tf_op jit(solution)/shard_map/ppermute | solution.py:16
  753.4 3.4 collective-permute-start.56
  756.8 83.6 %while.55 = (s32[]{:T(128)}, f32[512,128]{1,0:T(8,128)S(1)}, s32[16]{0:T(128)S(1)}, f32[3,512]{1,0:T(4,128)S(1)}, s32[]{:T(128)}, /*index=5*/f32[17,524,128]{2,1...) while((s32[]{:T(128)}, f32[512,128]{1,0:T(8,128)S(1)}, ...), condition=%wide.region_1.2_spmd.clone, body=%wide.region_0.1_spmd.clone.sunk | while | flops 405471232 | bytes 824088 | solution.py:45
  (371 shorter events, 236.1 us)
Async XLA Ops:
  2.5 34.0 %collective-permute-start.16 = (f32[131,128]{1,0:T(8,128)S(1)}, f32[131,128]{1,0:T(8,128)S(1)}, u32[]{:S(2)}, u32[]{:S(2)}) collective-permute-start(f32[131,128]{1,0:T(8,128)S(1)} %pad_maximum_fusion.1), channel_id=1, source_target_pairs={{0,8},{1,9},{2,10},{3,11},{4,12},{5,13},{6,14},{7,15},{8,16},{9,17... | collective-permute-start | bytes 201224 | tf_op jit(solution)/shard_map/ppermute | solution.py:22
  4.5 35.4 %collective-permute-start.17 = (f32[131,128]{1,0:T(8,128)S(1)}, f32[131,128]{1,0:T(8,128)S(1)}, u32[]{:S(2)}, u32[]{:S(2)}) collective-permute-start(f32[131,128]{1,0:T(8,128)S(1)} %pad_maximum_fusion.1), channel_id=1, source_target_pairs={{0,7},{1,8},{2,9},{3,10},{4,11},{5,12},{6,13},{7,14},{8,15},{9,16}... | collective-permute-start | bytes 201224 | tf_op jit(solution)/shard_map/ppermute | solution.py:22
  9.9 32.7 %collective-permute-start.18 = (f32[131,128]{1,0:T(8,128)S(1)}, f32[131,128]{1,0:T(8,128)S(1)}, u32[]{:S(2)}, u32[]{:S(2)}) collective-permute-start(f32[131,128]{1,0:T(8,128)S(1)} %pad_maximum_fusion.1), channel_id=1, source_target_pairs={{0,6},{1,7},{2,8},{3,9},{4,10},{5,11},{6,12},{7,13},{8,14},{9,15},... | collective-permute-start | bytes 201224 | tf_op jit(solution)/shard_map/ppermute | solution.py:22
  16.1 29.0 %collective-permute-start.19 = (f32[131,128]{1,0:T(8,128)S(1)}, f32[131,128]{1,0:T(8,128)S(1)}, u32[]{:S(2)}, u32[]{:S(2)}) collective-permute-start(f32[131,128]{1,0:T(8,128)S(1)} %pad_maximum_fusion.1), channel_id=1, source_target_pairs={{0,5},{1,6},{2,7},{3,8},{4,9},{5,10},{6,11},{7,12},{8,13},{9,14},{... | collective-permute-start | bytes 201224 | tf_op jit(solution)/shard_map/ppermute | solution.py:22
  32.3 14.8 %collective-permute-start.20 = (f32[131,128]{1,0:T(8,128)S(1)}, f32[131,128]{1,0:T(8,128)S(1)}, u32[]{:S(2)}, u32[]{:S(2)}) collective-permute-start(f32[131,128]{1,0:T(8,128)S(1)} %pad_maximum_fusion.1), channel_id=1, source_target_pairs={{0,4},{1,5},{2,6},{3,7},{4,8},{5,9},{6,10},{7,11},{8,12},{9,13},{1... | collective-permute-start | bytes 201224 | tf_op jit(solution)/shard_map/ppermute | solution.py:22
  36.5 14.4 %collective-permute-start.21 = (f32[131,128]{1,0:T(8,128)S(1)}, f32[131,128]{1,0:T(8,128)S(1)}, u32[]{:S(2)}, u32[]{:S(2)}) collective-permute-start(f32[131,128]{1,0:T(8,128)S(1)} %pad_maximum_fusion.1), channel_id=1, source_target_pairs={{0,3},{1,4},{2,5},{3,6},{4,7},{5,8},{6,9},{7,10},{8,11},{9,12},{10... | collective-permute-start | bytes 201224 | tf_op jit(solution)/shard_map/ppermute | solution.py:22
  39.8 15.0 %collective-permute-start.22 = (f32[131,128]{1,0:T(8,128)S(1)}, f32[131,128]{1,0:T(8,128)S(1)}, u32[]{:S(2)}, u32[]{:S(2)}) collective-permute-start(f32[131,128]{1,0:T(8,128)S(1)} %pad_maximum_fusion.1), channel_id=1, source_target_pairs={{0,2},{1,3},{2,4},{3,5},{4,6},{5,7},{6,8},{7,9},{8,10},{9,11},{10,... | collective-permute-start | bytes 201224 | tf_op jit(solution)/shard_map/ppermute | solution.py:22
  42.5 16.7 %collective-permute-start.23 = (f32[131,128]{1,0:T(8,128)S(1)}, f32[131,128]{1,0:T(8,128)S(1)}, u32[]{:S(2)}, u32[]{:S(2)}) collective-permute-start(f32[131,128]{1,0:T(8,128)S(1)} %pad_maximum_fusion.1), channel_id=1, source_target_pairs={{0,1},{1,2},{2,3},{3,4},{4,5},{5,6},{6,7},{7,8},{8,9},{9,10},{10,1... | collective-permute-start | bytes 201224 | tf_op jit(solution)/shard_map/ppermute | solution.py:22
  45.1 16.8 %collective-permute-start.24 = (f32[131,128]{1,0:T(8,128)S(1)}, f32[131,128]{1,0:T(8,128)S(1)}, u32[]{:S(2)}, u32[]{:S(2)}) collective-permute-start(f32[131,128]{1,0:T(8,128)S(1)} %pad_maximum_fusion.1), channel_id=1, source_target_pairs={{1,0},{2,1},{3,2},{4,3},{5,4},{6,5},{7,6},{8,7},{9,8},{10,9},{11,1... | collective-permute-start | bytes 201224 | tf_op jit(solution)/shard_map/ppermute | solution.py:22
  47.1 16.8 %collective-permute-start.25 = (f32[131,128]{1,0:T(8,128)S(1)}, f32[131,128]{1,0:T(8,128)S(1)}, u32[]{:S(2)}, u32[]{:S(2)}) collective-permute-start(f32[131,128]{1,0:T(8,128)S(1)} %pad_maximum_fusion.1), channel_id=1, source_target_pairs={{2,0},{3,1},{4,2},{5,3},{6,4},{7,5},{8,6},{9,7},{10,8},{11,9},{12,... | collective-permute-start | bytes 201224 | tf_op jit(solution)/shard_map/ppermute | solution.py:22
  51.0 18.7 %collective-permute-start.26 = (f32[131,128]{1,0:T(8,128)S(1)}, f32[131,128]{1,0:T(8,128)S(1)}, u32[]{:S(2)}, u32[]{:S(2)}) collective-permute-start(f32[131,128]{1,0:T(8,128)S(1)} %pad_maximum_fusion.1), channel_id=1, source_target_pairs={{3,0},{4,1},{5,2},{6,3},{7,4},{8,5},{9,6},{10,7},{11,8},{12,9},{13... | collective-permute-start | bytes 201224 | tf_op jit(solution)/shard_map/ppermute | solution.py:22
  54.9 20.8 %collective-permute-start.27 = (f32[131,128]{1,0:T(8,128)S(1)}, f32[131,128]{1,0:T(8,128)S(1)}, u32[]{:S(2)}, u32[]{:S(2)}) collective-permute-start(f32[131,128]{1,0:T(8,128)S(1)} %pad_maximum_fusion.1), channel_id=1, source_target_pairs={{4,0},{5,1},{6,2},{7,3},{8,4},{9,5},{10,6},{11,7},{12,8},{13,9},{1... | collective-permute-start | bytes 201224 | tf_op jit(solution)/shard_map/ppermute | solution.py:22
  59.2 25.9 %collective-permute-start.28 = (f32[131,128]{1,0:T(8,128)S(1)}, f32[131,128]{1,0:T(8,128)S(1)}, u32[]{:S(2)}, u32[]{:S(2)}) collective-permute-start(f32[131,128]{1,0:T(8,128)S(1)} %pad_maximum_fusion.1), channel_id=1, source_target_pairs={{5,0},{6,1},{7,2},{8,3},{9,4},{10,5},{11,6},{12,7},{13,8},{14,9},{... | collective-permute-start | bytes 201224 | tf_op jit(solution)/shard_map/ppermute | solution.py:22
  61.9 57.4 %collective-permute-start.29 = (f32[131,128]{1,0:T(8,128)S(1)}, f32[131,128]{1,0:T(8,128)S(1)}, u32[]{:S(2)}, u32[]{:S(2)}) collective-permute-start(f32[131,128]{1,0:T(8,128)S(1)} %pad_maximum_fusion.1), channel_id=1, source_target_pairs={{6,0},{7,1},{8,2},{9,3},{10,4},{11,5},{12,6},{13,7},{14,8},{15,9},... | collective-permute-start | bytes 201224 | tf_op jit(solution)/shard_map/ppermute | solution.py:22
  63.9 60.7 %collective-permute-start.30 = (f32[131,128]{1,0:T(8,128)S(1)}, f32[131,128]{1,0:T(8,128)S(1)}, u32[]{:S(2)}, u32[]{:S(2)}) collective-permute-start(f32[131,128]{1,0:T(8,128)S(1)} %pad_maximum_fusion.1), channel_id=1, source_target_pairs={{7,0},{8,1},{9,2},{10,3},{11,4},{12,5},{13,6},{14,7},{15,8},{16,9}... | collective-permute-start | bytes 201224 | tf_op jit(solution)/shard_map/ppermute | solution.py:22
  69.7 87.8 %collective-permute-start.31 = (f32[131,128]{1,0:T(8,128)S(1)}, f32[131,128]{1,0:T(8,128)S(1)}, u32[]{:S(2)}, u32[]{:S(2)}) collective-permute-start(f32[131,128]{1,0:T(8,128)S(1)} %pad_maximum_fusion.1), channel_id=1, source_target_pairs={{8,0},{9,1},{10,2},{11,3},{12,4},{13,5},{14,6},{15,7},{16,8},{17,9... | collective-permute-start | bytes 201224 | tf_op jit(solution)/shard_map/ppermute | solution.py:22
  78.9 512.4 %collective-permute-start = (f32[524,128]{1,0:T(8,128)S(1)}, f32[524,128]{1,0:T(8,128)S(1)}, u32[]{:S(2)}, u32[]{:S(2)}) collective-permute-start(f32[524,128]{1,0:T(8,128)S(1)} %pad_maximum_fusion), channel_id=1, source_target_pairs={{0,8},{1,9},{2,10},{3,11},{4,12},{5,13},{6,14},{7,15},{8,16},{9,17... | collective-permute-start | bytes 804872 | tf_op jit(solution)/shard_map/ppermute | solution.py:22
  85.1 32.0 %collective-permute-start.42 = (f32[128,128]{1,0:T(8,128)S(1)}, f32[128,128]{1,0:T(8,128)S(1)}, u32[]{:S(2)}, u32[]{:S(2)}) collective-permute-start(f32[128,128]{1,0:T(8,128)S(1)} %add.193), channel_id=1, source_target_pairs={{0,2},{1,3},{2,0},{3,1},{4,6},{5,7},{6,4},{7,5},{8,10},{9,11},{10,... | collective-permute-start | bytes 196616 | tf_op jit(solution)/shard_map/ppermute | solution.py:16
  117.1 491.3 %collective-permute-start.1 = (f32[524,128]{1,0:T(8,128)S(1)}, f32[524,128]{1,0:T(8,128)S(1)}, u32[]{:S(2)}, u32[]{:S(2)}) collective-permute-start(f32[524,128]{1,0:T(8,128)S(1)} %pad_maximum_fusion), channel_id=1, source_target_pairs={{0,7},{1,8},{2,9},{3,10},{4,11},{5,12},{6,13},{7,14},{8,15},{9,16}... | collective-permute-start | bytes 804872 | tf_op jit(solution)/shard_map/ppermute | solution.py:22
  122.6 492.9 %collective-permute-start.2 = (f32[524,128]{1,0:T(8,128)S(1)}, f32[524,128]{1,0:T(8,128)S(1)}, u32[]{:S(2)}, u32[]{:S(2)}) collective-permute-start(f32[524,128]{1,0:T(8,128)S(1)} %pad_maximum_fusion), channel_id=1, source_target_pairs={{0,6},{1,7},{2,8},{3,9},{4,10},{5,11},{6,12},{7,13},{8,14},{9,15},... | collective-permute-start | bytes 804872 | tf_op jit(solution)/shard_map/ppermute | solution.py:22
  124.5 18.7 %collective-permute-start.52 = (f32[128,128]{1,0:T(8,128)S(1)}, f32[128,128]{1,0:T(8,128)S(1)}, u32[]{:S(2)}, u32[]{:S(2)}) collective-permute-start(f32[128,128]{1,0:T(8,128)S(1)} %add.196), channel_id=1, source_target_pairs={{0,2},{1,3},{2,0},{3,1},{4,6},{5,7},{6,4},{7,5},{8,10},{9,11},{10,... | collective-permute-start | bytes 196616 | tf_op jit(solution)/shard_map/ppermute | solution.py:16
  143.3 475.1 %collective-permute-start.3 = (f32[524,128]{1,0:T(8,128)S(1)}, f32[524,128]{1,0:T(8,128)S(1)}, u32[]{:S(2)}, u32[]{:S(2)}) collective-permute-start(f32[524,128]{1,0:T(8,128)S(1)} %pad_maximum_fusion), channel_id=1, source_target_pairs={{0,5},{1,6},{2,7},{3,8},{4,9},{5,10},{6,11},{7,12},{8,13},{9,14},{... | collective-permute-start | bytes 804872 | tf_op jit(solution)/shard_map/ppermute | solution.py:22
  157.5 16.3 %collective-permute-start.53 = (f32[128,128]{1,0:T(8,128)S(1)}, f32[128,128]{1,0:T(8,128)S(1)}, u32[]{:S(2)}, u32[]{:S(2)}) collective-permute-start(f32[128,128]{1,0:T(8,128)S(1)} %add.197), channel_id=1, source_target_pairs={{0,4},{1,5},{2,6},{3,7},{4,0},{5,1},{6,2},{7,3},{8,12},{9,13},{10,... | collective-permute-start | bytes 196616 | tf_op jit(solution)/shard_map/ppermute | solution.py:16
  173.8 64.7 %collective-permute-start.33 = (f32[128,128]{1,0:T(8,128)S(1)}, f32[128,128]{1,0:T(8,128)S(1)}, u32[]{:S(2)}, u32[]{:S(2)}) collective-permute-start(f32[128,128]{1,0:T(8,128)S(1)} %add.188), channel_id=1, source_target_pairs={{0,8},{1,9},{2,10},{3,11},{4,12},{5,13},{6,14},{7,15},{8,16},{9,17... | collective-permute-start | bytes 196616 | tf_op jit(solution)/shard_map/ppermute | solution.py:22
  178.1 520.4 %all-to-all-start = ((f32[512,16,128]{2,1,0:T(8,128)}), f32[512,16,128]{2,1,0:T(8,128)}, u32[]{:S(2)}, u32[]{:S(2)}) async-start(f32[512,16,128]{2,1,0:T(8,128)} %stack.164), calls=%async_computation | async-start | bytes 8388608 | tf_op jit(solution)/shard_map/all_to_all | solution.py:163
  238.5 151.5 %collective-permute-start.34 = (f32[128,128]{1,0:T(8,128)S(1)}, f32[128,128]{1,0:T(8,128)S(1)}, u32[]{:S(2)}, u32[]{:S(2)}) collective-permute-start(f32[128,128]{1,0:T(8,128)S(1)} %add.188), channel_id=1, source_target_pairs={{0,6},{1,7},{2,8},{3,9},{4,10},{5,11},{6,12},{7,13},{8,14},{9,15},... | collective-permute-start | bytes 196616 | tf_op jit(solution)/shard_map/ppermute | solution.py:22
  415.4 16.3 %collective-permute-start.39 = (f32[128,128]{1,0:T(8,128)S(1)}, f32[128,128]{1,0:T(8,128)S(1)}, u32[]{:S(2)}, u32[]{:S(2)}) collective-permute-start(f32[128,128]{1,0:T(8,128)S(1)} %add.188), channel_id=1, source_target_pairs={{6,0},{7,1},{8,2},{9,3},{10,4},{11,5},{12,6},{13,7},{14,8},{15,9},... | collective-permute-start | bytes 196616 | tf_op jit(solution)/shard_map/ppermute | solution.py:22
  431.7 11.9 %collective-permute-start.40 = (f32[128,128]{1,0:T(8,128)S(1)}, f32[128,128]{1,0:T(8,128)S(1)}, u32[]{:S(2)}, u32[]{:S(2)}) collective-permute-start(f32[128,128]{1,0:T(8,128)S(1)} %add.188), channel_id=1, source_target_pairs={{8,0},{9,1},{10,2},{11,3},{12,4},{13,5},{14,6},{15,7},{16,8},{17,9... | collective-permute-start | bytes 196616 | tf_op jit(solution)/shard_map/ppermute | solution.py:22
  443.6 25.4 %collective-permute-start.43 = (f32[128,128]{1,0:T(8,128)S(1)}, f32[128,128]{1,0:T(8,128)S(1)}, u32[]{:S(2)}, u32[]{:S(2)}) collective-permute-start(f32[128,128]{1,0:T(8,128)S(1)} %add.194), channel_id=1, source_target_pairs={{0,16},{1,17},{2,18},{3,19},{4,20},{5,21},{6,22},{7,23},{8,24},{9,... | collective-permute-start | bytes 196616 | tf_op jit(solution)/shard_map/ppermute | solution.py:22
  469.0 13.6 %collective-permute-start.44 = (f32[128,128]{1,0:T(8,128)S(1)}, f32[128,128]{1,0:T(8,128)S(1)}, u32[]{:S(2)}, u32[]{:S(2)}) collective-permute-start(f32[128,128]{1,0:T(8,128)S(1)} %add.194), channel_id=1, source_target_pairs={{0,12},{1,13},{2,14},{3,15},{4,16},{5,17},{6,18},{7,19},{8,20},{9,... | collective-permute-start | bytes 196616 | tf_op jit(solution)/shard_map/ppermute | solution.py:22
  482.7 12.1 %collective-permute-start.45 = (f32[128,128]{1,0:T(8,128)S(1)}, f32[128,128]{1,0:T(8,128)S(1)}, u32[]{:S(2)}, u32[]{:S(2)}) collective-permute-start(f32[128,128]{1,0:T(8,128)S(1)} %add.194), channel_id=1, source_target_pairs={{0,8},{1,9},{2,10},{3,11},{4,12},{5,13},{6,14},{7,15},{8,16},{9,17... | collective-permute-start | bytes 196616 | tf_op jit(solution)/shard_map/ppermute | solution.py:22
  511.0 13.0 %collective-permute-start.48 = (f32[128,128]{1,0:T(8,128)S(1)}, f32[128,128]{1,0:T(8,128)S(1)}, u32[]{:S(2)}, u32[]{:S(2)}) collective-permute-start(f32[128,128]{1,0:T(8,128)S(1)} %add.194), channel_id=1, source_target_pairs={{8,0},{9,1},{10,2},{11,3},{12,4},{13,5},{14,6},{15,7},{16,8},{17,9... | collective-permute-start | bytes 196616 | tf_op jit(solution)/shard_map/ppermute | solution.py:22
  524.0 13.8 %collective-permute-start.49 = (f32[128,128]{1,0:T(8,128)S(1)}, f32[128,128]{1,0:T(8,128)S(1)}, u32[]{:S(2)}, u32[]{:S(2)}) collective-permute-start(f32[128,128]{1,0:T(8,128)S(1)} %add.194), channel_id=1, source_target_pairs={{12,0},{13,1},{14,2},{15,3},{16,4},{17,5},{18,6},{19,7},{20,8},{21... | collective-permute-start | bytes 196616 | tf_op jit(solution)/shard_map/ppermute | solution.py:22
  537.8 16.7 %collective-permute-start.50 = (f32[128,128]{1,0:T(8,128)S(1)}, f32[128,128]{1,0:T(8,128)S(1)}, u32[]{:S(2)}, u32[]{:S(2)}) collective-permute-start(f32[128,128]{1,0:T(8,128)S(1)} %add.194), channel_id=1, source_target_pairs={{16,0},{17,1},{18,2},{19,3},{20,4},{21,5},{22,6},{23,7},{24,8},{25... | collective-permute-start | bytes 196616 | tf_op jit(solution)/shard_map/ppermute | solution.py:22
  554.5 66.9 %collective-permute-start.4 = (f32[524,128]{1,0:T(8,128)S(1)}, f32[524,128]{1,0:T(8,128)S(1)}, u32[]{:S(2)}, u32[]{:S(2)}) collective-permute-start(f32[524,128]{1,0:T(8,128)S(1)} %pad_maximum_fusion), channel_id=1, source_target_pairs={{0,4},{1,5},{2,6},{3,7},{4,8},{5,9},{6,10},{7,11},{8,12},{9,13},{1... | collective-permute-start | bytes 804872 | tf_op jit(solution)/shard_map/ppermute | solution.py:22
  591.3 35.3 %collective-permute-start.5 = (f32[524,128]{1,0:T(8,128)S(1)}, f32[524,128]{1,0:T(8,128)S(1)}, u32[]{:S(2)}, u32[]{:S(2)}) collective-permute-start(f32[524,128]{1,0:T(8,128)S(1)} %pad_maximum_fusion), channel_id=1, source_target_pairs={{0,3},{1,4},{2,5},{3,6},{4,7},{5,8},{6,9},{7,10},{8,11},{9,12},{10... | collective-permute-start | bytes 804872 | tf_op jit(solution)/shard_map/ppermute | solution.py:22
  608.4 22.4 %collective-permute-start.6 = (f32[524,128]{1,0:T(8,128)S(1)}, f32[524,128]{1,0:T(8,128)S(1)}, u32[]{:S(2)}, u32[]{:S(2)}) collective-permute-start(f32[524,128]{1,0:T(8,128)S(1)} %pad_maximum_fusion), channel_id=1, source_target_pairs={{0,2},{1,3},{2,4},{3,5},{4,6},{5,7},{6,8},{7,9},{8,10},{9,11},{10,... | collective-permute-start | bytes 804872 | tf_op jit(solution)/shard_map/ppermute | solution.py:22
  615.5 18.1 %collective-permute-start.7 = (f32[524,128]{1,0:T(8,128)S(1)}, f32[524,128]{1,0:T(8,128)S(1)}, u32[]{:S(2)}, u32[]{:S(2)}) collective-permute-start(f32[524,128]{1,0:T(8,128)S(1)} %pad_maximum_fusion), channel_id=1, source_target_pairs={{0,1},{1,2},{2,3},{3,4},{4,5},{5,6},{6,7},{7,8},{8,9},{9,10},{10,1... | collective-permute-start | bytes 804872 | tf_op jit(solution)/shard_map/ppermute | solution.py:22
  618.4 18.6 %collective-permute-start.8 = (f32[524,128]{1,0:T(8,128)S(1)}, f32[524,128]{1,0:T(8,128)S(1)}, u32[]{:S(2)}, u32[]{:S(2)}) collective-permute-start(f32[524,128]{1,0:T(8,128)S(1)} %pad_maximum_fusion), channel_id=1, source_target_pairs={{1,0},{2,1},{3,2},{4,3},{5,4},{6,5},{7,6},{8,7},{9,8},{10,9},{11,1... | collective-permute-start | bytes 804872 | tf_op jit(solution)/shard_map/ppermute | solution.py:22
  621.4 18.2 %collective-permute-start.9 = (f32[524,128]{1,0:T(8,128)S(1)}, f32[524,128]{1,0:T(8,128)S(1)}, u32[]{:S(2)}, u32[]{:S(2)}) collective-permute-start(f32[524,128]{1,0:T(8,128)S(1)} %pad_maximum_fusion), channel_id=1, source_target_pairs={{2,0},{3,1},{4,2},{5,3},{6,4},{7,5},{8,6},{9,7},{10,8},{11,9},{12,... | collective-permute-start | bytes 804872 | tf_op jit(solution)/shard_map/ppermute | solution.py:22
  626.6 15.7 %collective-permute-start.10 = (f32[524,128]{1,0:T(8,128)S(1)}, f32[524,128]{1,0:T(8,128)S(1)}, u32[]{:S(2)}, u32[]{:S(2)}) collective-permute-start(f32[524,128]{1,0:T(8,128)S(1)} %pad_maximum_fusion), channel_id=1, source_target_pairs={{3,0},{4,1},{5,2},{6,3},{7,4},{8,5},{9,6},{10,7},{11,8},{12,9},{13... | collective-permute-start | bytes 804872 | tf_op jit(solution)/shard_map/ppermute | solution.py:22
  630.8 18.0 %collective-permute-start.11 = (f32[524,128]{1,0:T(8,128)S(1)}, f32[524,128]{1,0:T(8,128)S(1)}, u32[]{:S(2)}, u32[]{:S(2)}) collective-permute-start(f32[524,128]{1,0:T(8,128)S(1)} %pad_maximum_fusion), channel_id=1, source_target_pairs={{4,0},{5,1},{6,2},{7,3},{8,4},{9,5},{10,6},{11,7},{12,8},{13,9},{1... | collective-permute-start | bytes 804872 | tf_op jit(solution)/shard_map/ppermute | solution.py:22
  633.6 58.7 %collective-permute-start.12 = (f32[524,128]{1,0:T(8,128)S(1)}, f32[524,128]{1,0:T(8,128)S(1)}, u32[]{:S(2)}, u32[]{:S(2)}) collective-permute-start(f32[524,128]{1,0:T(8,128)S(1)} %pad_maximum_fusion), channel_id=1, source_target_pairs={{5,0},{6,1},{7,2},{8,3},{9,4},{10,5},{11,6},{12,7},{13,8},{14,9},{... | collective-permute-start | bytes 804872 | tf_op jit(solution)/shard_map/ppermute | solution.py:22
  636.9 60.8 %collective-permute-start.13 = (f32[524,128]{1,0:T(8,128)S(1)}, f32[524,128]{1,0:T(8,128)S(1)}, u32[]{:S(2)}, u32[]{:S(2)}) collective-permute-start(f32[524,128]{1,0:T(8,128)S(1)} %pad_maximum_fusion), channel_id=1, source_target_pairs={{6,0},{7,1},{8,2},{9,3},{10,4},{11,5},{12,6},{13,7},{14,8},{15,9},... | collective-permute-start | bytes 804872 | tf_op jit(solution)/shard_map/ppermute | solution.py:22
  639.6 108.1 %collective-permute-start.14 = (f32[524,128]{1,0:T(8,128)S(1)}, f32[524,128]{1,0:T(8,128)S(1)}, u32[]{:S(2)}, u32[]{:S(2)}) collective-permute-start(f32[524,128]{1,0:T(8,128)S(1)} %pad_maximum_fusion), channel_id=1, source_target_pairs={{7,0},{8,1},{9,2},{10,3},{11,4},{12,5},{13,6},{14,7},{15,8},{16,9}... | collective-permute-start | bytes 804872 | tf_op jit(solution)/shard_map/ppermute | solution.py:22
  642.3 108.2 %collective-permute-start.15 = (f32[524,128]{1,0:T(8,128)S(1)}, f32[524,128]{1,0:T(8,128)S(1)}, u32[]{:S(2)}, u32[]{:S(2)}) collective-permute-start(f32[524,128]{1,0:T(8,128)S(1)} %pad_maximum_fusion), channel_id=1, source_target_pairs={{8,0},{9,1},{10,2},{11,3},{12,4},{13,5},{14,6},{15,7},{16,8},{17,9... | collective-permute-start | bytes 804872 | tf_op jit(solution)/shard_map/ppermute | solution.py:22
  727.3 21.2 %collective-permute-start.54 = (f32[32,128]{1,0:T(8,128)S(1)}, f32[32,128]{1,0:T(8,128)S(1)}, u32[]{:S(2)}, u32[]{:S(2)}) collective-permute-start(f32[32,128]{1,0:T(8,128)S(1)} %add.201), channel_id=1, source_target_pairs={{0,1},{1,0},{2,3},{3,2},{4,5},{5,4},{6,7},{7,6},{8,9},{9,8},{10,11... | collective-permute-start | bytes 49160 | tf_op jit(solution)/shard_map/ppermute | solution.py:16
  753.4 87.2 %collective-permute-start.56 = (f32[64,128]{1,0:T(8,128)S(1)}, f32[64,128]{1,0:T(8,128)S(1)}, u32[]{:S(2)}, u32[]{:S(2)}) collective-permute-start(f32[64,128]{1,0:T(8,128)S(1)} %add.202), channel_id=1, source_target_pairs={{0,1},{1,0},{2,3},{3,2},{4,5},{5,4},{6,7},{7,6},{8,9},{9,8},{10,11... | collective-permute-start | bytes 98312 | tf_op jit(solution)/shard_map/ppermute | solution.py:16
  (18 other events, 761.0 us)
